TPU v7x, 512 devices: a whole 4x4x16 slice. The times are simulated.
512 devices in a mesh: rows: 128 (over x, z_lo, y), feat: 4 (over z_hi, core).
Axes of the slice: x: 4, y: 4, z: 16 (z_hi: 2, z_lo: 8; z = z_hi * 8 + z_lo), core: 2. Of those that a mesh axis runs over, the one named last changes fastest.
Arguments:
- features: bfloat16 [32768, 512], P('rows', 'feat'), may hold values from -6 to 6
- weight: bfloat16 [512, 512], P(None, 'feat'), may hold values from -0.25 to 0.25
- block_values: bfloat16 [256, 8, 128, 128], P('rows', 'feat'), may hold values from -0.25 to 0.25
- columns: int32 [256, 8], P('rows'), may hold values from 0 to 255, as said below
- counts: int32 [256], P('rows'), may hold values from 2 to 8, as said below
- cotangent: bfloat16 [32768, 512], P('rows', 'feat'), may hold values from -6 to 6
Outputs:
- hidden: bfloat16 [32768, 512], P('rows', 'feat')
- grad_features: bfloat16 [32768, 512], P('rows', 'feat')
- grad_weight: float32 [512, 512], P(None, 'feat')
Inputs may be any that keep to these rules, and one draw needn't show every extreme that they name: `columns`: the 8 column blocks of a row block are distinct and lie on the devices within 4 indices of the row block's own index along rows, counted around the axis (the device of block c is c // 2). Slots 0 to counts[g] - 1 of row block g are live, the others are ignored; some row block has exactly 8 live slots.
All inputs are finite; a program needn't handle non-finite values.
Results may differ from a plain program's by a relative error of at most 0.0067.
Values may be sent and summed in bfloat16 or wider, within the bound.
No kernel may reach another device: no remote copies, remote signals or barrier semaphores. Data moves between devices by JAX's collectives and lax.ppermute only.
A program may use at most 64 MiB of HBM per device.

v0:
```python
import jax
import jax.numpy as jnp
from jax import lax
from jax.sharding import PartitionSpec as P


def shifted(value, axis, steps):
    count = lax.axis_size(axis)
    pairs = [(source, (source + steps) % count) for source in range(count)]
    return lax.ppermute(value, axis, pairs)


def activation(values):
    return jax.nn.gelu(values, approximate=True)


def window_index(columns, row_blocks, center, halo_reach, row_count):
    owner_dev = columns // row_blocks
    offset = (owner_dev - center + halo_reach + row_count) % row_count
    return offset * row_blocks + columns % row_blocks


def live_tiles(panel_part, first_slot, counts, places):
    slot_count = panel_part.shape[1]
    slot_ids = first_slot + jnp.arange(slot_count)
    slot_live = counts[:, None] > slot_ids[None, :]
    tiles = jnp.where(slot_live[:, :, None, None], panel_part, jnp.zeros((), panel_part.dtype))
    return (tiles, places)


def gather_slots(panel_part, first_slot, counts, places, window):
    tiles, targets = live_tiles(panel_part, first_slot, counts, places)
    picked = jnp.take(window, targets, axis=0)
    product = jnp.einsum("gsij,gsjf->gif", tiles, picked, preferred_element_type=jnp.float32)
    return product


def spread_slots(running, panel_part, first_slot, counts, places, grad_blocks):
    tiles, targets = live_tiles(panel_part, first_slot, counts, places)
    block_size = grad_blocks.shape[1]
    feat_width = grad_blocks.shape[2]
    product = jnp.einsum("gsij,gif->gsjf", tiles, grad_blocks, preferred_element_type=jnp.float32)
    return running.at[targets.reshape(-1)].add(product.reshape(-1, block_size, feat_width))


def on_device(features, weight, block_values, columns, counts, cotangent):
    row_count = lax.axis_size("rows")
    center = lax.axis_index("rows")
    halo_reach = min(4, (row_count - 1) // 3)
    row_blocks = counts.shape[0]
    block_size = block_values.shape[2]
    feat_width = features.shape[1]
    local_rows = features.shape[0]
    span_blocks = (2 * halo_reach + 1) * row_blocks
    pieces = {0: features}
    for offset in list(range(-halo_reach, 0)) + list(range(1, halo_reach + 1)):
        pieces[offset] = shifted(features, "rows", -offset)
    window = jnp.stack([pieces[offset] for offset in range(-halo_reach, halo_reach + 1)])
    window = window.reshape(span_blocks, block_size, feat_width)
    places = window_index(columns, row_blocks, center, halo_reach, row_count)
    panel_full = lax.all_gather(block_values, "feat", axis=1, tiled=True)
    summed = gather_slots(panel_full, 0, counts, places, window)
    aggregated = summed.reshape(local_rows, feat_width).astype(jnp.bfloat16)
    agg_full, weight_full = (
        lax.all_gather(aggregated, "feat", axis=1, tiled=True),
        lax.all_gather(weight, "feat", axis=1, tiled=True),
    )
    pre_act = jnp.dot(agg_full, weight, preferred_element_type=jnp.float32)
    hidden, act_grad = jax.vjp(activation, pre_act)
    grad_pre = act_grad(cotangent.astype(jnp.float32))[0].astype(jnp.bfloat16)
    grad_full = lax.all_gather(grad_pre, "feat", axis=1, tiled=True)
    weight_terms = lax.dot_general(
        agg_full, grad_pre, (((0,), (0,)), ((), ())), preferred_element_type=jnp.float32
    )
    node_total = local_rows * row_count
    grad_weight = lax.psum(weight_terms, "rows") * float(node_total) ** (-0.5)
    feat_index = lax.axis_index("feat")
    weight_rows = lax.dynamic_slice_in_dim(weight_full, feat_index * feat_width, feat_width, 0)
    grad_agg = lax.dot_general(
        grad_full, weight_rows, (((1,), (1,)), ((), ())), preferred_element_type=jnp.float32
    )
    grad_blocks = grad_agg.astype(jnp.bfloat16).reshape(row_blocks, block_size, feat_width)
    zero_window = jnp.zeros((span_blocks, block_size, feat_width), jnp.float32)
    spread = spread_slots(zero_window, panel_full, 0, counts, places, grad_blocks)
    spread = spread.reshape(2 * halo_reach + 1, local_rows, feat_width)
    grad_local = spread[halo_reach]
    for offset in list(range(-halo_reach, 0)) + list(range(1, halo_reach + 1)):
        outgoing = spread[halo_reach + offset].astype(jnp.bfloat16)
        arrived = shifted(outgoing, "rows", offset)
        grad_local = grad_local + arrived.astype(jnp.float32)
    return (hidden.astype(jnp.bfloat16), grad_local.astype(jnp.bfloat16), grad_weight)


def solution(mesh):
    in_specs = (
        P("rows", "feat"),
        P(None, "feat"),
        P("rows", "feat", None, None),
        P("rows", None),
        P("rows"),
        P("rows", "feat"),
    )
    out_specs = (P("rows", "feat"), P("rows", "feat"), P(None, "feat"))
    return jax.shard_map(
        on_device, mesh=mesh, in_specs=in_specs, out_specs=out_specs, check_vma=False
    )
```

profile of v0, /device:TPU:0, one launch (start us, length us, event | category | flops | bytes accessed | tf_op | source)
XLA Modules:
  0.0 2029.0 jit_solution(9673792675788454822)
XLA Ops:
  7.2 0.0 copy-start.1
  7.2 0.0 all-reduce.2.cloned.1.call-start
  7.2 12.6 collective-permute-start.5
  19.9 3.0 collective-permute-start.4
  22.8 2.9 collective-permute-start.3
  25.7 2.6 collective-permute-start.2
  28.4 1.9 collective-permute-start
  30.3 0.7 compare_and_fusion
  31.0 0.1 reshape.102
  31.1 0.7 iota_compare_fusion
  31.8 0.1 reshape.107
  31.9 20.9 %all_gather.12 = bf16[2,8,128,128]{3,2,1,0:T(8,128)(2,1)S(1)} all-gather(bf16[2,2,128,128]{3,2,1,0:T(8,128)(2,1)} %param.8), channel_id=1, replica_groups=mesh['rows'=128,'feat'=4] {'feat'}, dimensions={1}, use_global_device_ids=true | all-gather | bytes 655360 | tf_op jit(solution)/shard_map/all_gather | solution.py:61
  52.8 20.9 %all_gather.15 = bf16[512,512]{1,0:T(8,128)(2,1)S(1)} all-gather(bf16[512,128]{1,0:T(8,128)(2,1)} %param.7), channel_id=1, replica_groups=mesh['rows'=128,'feat'=4] {'feat'}, dimensions={1}, use_global_device_ids=true | all-gather | bytes 655360 | tf_op jit(solution)/shard_map/all_gather | solution.py:66
  73.7 0.0 collective-permute-done
  73.7 0.0 copy-done.1
  73.7 1.9 collective-permute-start.1
  75.7 14.1 collective-permute-done.1
  89.7 1.9 collective-permute-start.7
  91.7 0.0 collective-permute-done.2
  91.7 2.0 collective-permute-start.6
  93.7 0.0 collective-permute-done.3
  93.7 0.0 collective-permute-done.4
  93.7 0.0 collective-permute-done.5
  93.8 5.3 collective-permute-done.6
  99.1 0.0 collective-permute-done.7
  99.1 0.6 gather_fusion
  99.8 0.0 copy-start
  99.8 0.0 copy-start.2
  99.8 0.4 fusion
  100.2 15.2 all_gather.13
  115.4 0.0 copy-done
  115.4 0.0 copy-done.2
  115.4 0.9 fusion.9
  116.3 14.6 all_gather.14
  130.9 0.2 convolution_convert_fusion
  131.2 0.4 fusion.3
  131.6 0.1 broadcast_in_dim.43
  131.7 1.6 scatter_fusion
  133.3 0.1 convert.10
  133.5 3.3 collective-permute-start.15
  136.8 11.3 collective-permute-start.8
  148.1 5.2 collective-permute-start.14
  153.2 3.1 collective-permute-start.13
  156.3 1.9 collective-permute-start.12
  158.2 0.0 collective-permute-done.15
  158.2 14.7 collective-permute-start.11
  173.0 0.0 collective-permute-done.8
  173.0 3.1 collective-permute-start.10
  176.1 0.0 collective-permute-done.14
  176.1 3.9 collective-permute-start.9
  180.0 1.0 fusion.36
  180.9 0.0 all-reduce.2.cloned.1.call-update
  181.0 0.0 collective-permute-done.13
  181.0 0.0 collective-permute-done.12
  181.0 0.0 collective-permute-done.11
  181.0 0.0 collective-permute-done.10
  181.0 2.4 collective-permute-done.9
  183.5 0.7 fusion.24
  184.2 1836.3 %all-reduce.2.cloned.1.call-done = f32[512,128]{1,0:T(8,128)} async-done(((f32[512,128]{1,0:T(8,128)}), f32[512,128]{1,0:T(8,128)}) %all-reduce.2.cloned.1.call-update) | async-done | bytes 262160 | tf_op jit(solution)/shard_map/psum | solution.py:76
  2020.5 1.7 broadcast_multiply_fusion
  (14 shorter events, 0.2 us)
Async XLA Ops:
  7.2 66.6 %copy-start.1 = (bf16[256,128]{1,0:T(8,128)(2,1)S(1)}, bf16[256,128]{1,0:T(8,128)(2,1)}, u32[]{:S(2)}) copy-start(bf16[256,128]{1,0:T(8,128)(2,1)} %param.6) | copy-start | bytes 196612
  7.2 2013.3 %all-reduce.2.cloned.1.call-start = ((), (), s32[]{:S(2)}) async-start(), calls=%async_computation | async-start | bytes 524288 | tf_op jit(solution)/shard_map/psum | solution.py:76
  7.2 86.5 %collective-permute-start.5 = (bf16[256,128]{1,0:T(8,128)(2,1)}, bf16[256,128]{1,0:T(8,128)(2,1)S(1)}, u32[]{:S(2)}, u32[]{:S(2)}) collective-permute-start(bf16[256,128]{1,0:T(8,128)(2,1)} %param.6), channel_id=1, source_target_pairs={{0,504},{4,508},{8,0},{12,4},{16,8},{20,12},{24,16},{28,20},{32,24... | collective-permute-start | bytes 196616 | tf_op jit(solution)/shard_map/ppermute | solution.py:10
  19.9 73.9 %collective-permute-start.4 = (bf16[256,128]{1,0:T(8,128)(2,1)}, bf16[256,128]{1,0:T(8,128)(2,1)S(1)}, u32[]{:S(2)}, u32[]{:S(2)}) collective-permute-start(bf16[256,128]{1,0:T(8,128)(2,1)} %param.6), channel_id=1, source_target_pairs={{0,508},{4,0},{8,4},{12,8},{16,12},{20,16},{24,20},{28,24},{32,28}... | collective-permute-start | bytes 196616 | tf_op jit(solution)/shard_map/ppermute | solution.py:10
  22.8 70.8 %collective-permute-start.3 = (bf16[256,128]{1,0:T(8,128)(2,1)}, bf16[256,128]{1,0:T(8,128)(2,1)S(1)}, u32[]{:S(2)}, u32[]{:S(2)}) collective-permute-start(bf16[256,128]{1,0:T(8,128)(2,1)} %param.6), channel_id=1, source_target_pairs={{0,4},{4,8},{8,12},{12,16},{16,20},{20,24},{24,28},{28,32},{32,36}... | collective-permute-start | bytes 196616 | tf_op jit(solution)/shard_map/ppermute | solution.py:10
  25.7 66.0 %collective-permute-start.2 = (bf16[256,128]{1,0:T(8,128)(2,1)}, bf16[256,128]{1,0:T(8,128)(2,1)S(1)}, u32[]{:S(2)}, u32[]{:S(2)}) collective-permute-start(bf16[256,128]{1,0:T(8,128)(2,1)} %param.6), channel_id=1, source_target_pairs={{0,8},{4,12},{8,16},{12,20},{16,24},{20,28},{24,32},{28,36},{32,40... | collective-permute-start | bytes 196616 | tf_op jit(solution)/shard_map/ppermute | solution.py:10
  28.4 45.4 %collective-permute-start = (bf16[256,128]{1,0:T(8,128)(2,1)}, bf16[256,128]{1,0:T(8,128)(2,1)S(1)}, u32[]{:S(2)}, u32[]{:S(2)}) collective-permute-start(bf16[256,128]{1,0:T(8,128)(2,1)} %param.6), channel_id=1, source_target_pairs={{0,16},{4,20},{8,24},{12,28},{16,32},{20,36},{24,40},{28,44},{32,4... | collective-permute-start | bytes 196616 | tf_op jit(solution)/shard_map/ppermute | solution.py:10
  73.7 16.0 collective-permute-start.1
  89.7 9.3 collective-permute-start.7
  91.7 7.4 collective-permute-start.6
  99.8 15.6 copy-start
  99.8 15.6 copy-start.2
  133.5 24.7 %collective-permute-start.15 = (bf16[256,128]{1,0:T(8,128)(2,1)S(1)}, bf16[256,128]{1,0:T(8,128)(2,1)S(1)}, u32[]{:S(2)}, u32[]{:S(2)}) collective-permute-start(bf16[256,128]{1,0:T(8,128)(2,1)S(1)} %bitcast.77), channel_id=1, source_target_pairs={{0,16},{4,20},{8,24},{12,28},{16,32},{20,36},{24,40},{28,44},{32,4... | collective-permute-start | bytes 196616 | tf_op jit(solution)/shard_map/ppermute | solution.py:10
  136.8 36.2 %collective-permute-start.8 = (bf16[256,128]{1,0:T(8,128)(2,1)S(1)}, bf16[256,128]{1,0:T(8,128)(2,1)S(1)}, u32[]{:S(2)}, u32[]{:S(2)}) collective-permute-start(bf16[256,128]{1,0:T(8,128)(2,1)S(1)} %bitcast.76), channel_id=1, source_target_pairs={{0,496},{4,500},{8,504},{12,508},{16,0},{20,4},{24,8},{28,12},{32,... | collective-permute-start | bytes 196616 | tf_op jit(solution)/shard_map/ppermute | solution.py:10
  148.1 28.0 %collective-permute-start.14 = (bf16[256,128]{1,0:T(8,128)(2,1)S(1)}, bf16[256,128]{1,0:T(8,128)(2,1)S(1)}, u32[]{:S(2)}, u32[]{:S(2)}) collective-permute-start(bf16[256,128]{1,0:T(8,128)(2,1)S(1)} %bitcast.75), channel_id=1, source_target_pairs={{0,12},{4,16},{8,20},{12,24},{16,28},{20,32},{24,36},{28,40},{32,4... | collective-permute-start | bytes 196616 | tf_op jit(solution)/shard_map/ppermute | solution.py:10
  153.2 27.8 %collective-permute-start.13 = (bf16[256,128]{1,0:T(8,128)(2,1)S(1)}, bf16[256,128]{1,0:T(8,128)(2,1)S(1)}, u32[]{:S(2)}, u32[]{:S(2)}) collective-permute-start(bf16[256,128]{1,0:T(8,128)(2,1)S(1)} %bitcast.74), channel_id=1, source_target_pairs={{0,8},{4,12},{8,16},{12,20},{16,24},{20,28},{24,32},{28,36},{32,40... | collective-permute-start | bytes 196616 | tf_op jit(solution)/shard_map/ppermute | solution.py:10
  156.3 24.7 %collective-permute-start.12 = (bf16[256,128]{1,0:T(8,128)(2,1)S(1)}, bf16[256,128]{1,0:T(8,128)(2,1)S(1)}, u32[]{:S(2)}, u32[]{:S(2)}) collective-permute-start(bf16[256,128]{1,0:T(8,128)(2,1)S(1)} %bitcast.73), channel_id=1, source_target_pairs={{0,4},{4,8},{8,12},{12,16},{16,20},{20,24},{24,28},{28,32},{32,36}... | collective-permute-start | bytes 196616 | tf_op jit(solution)/shard_map/ppermute | solution.py:10
  158.2 22.8 %collective-permute-start.11 = (bf16[256,128]{1,0:T(8,128)(2,1)S(1)}, bf16[256,128]{1,0:T(8,128)(2,1)S(1)}, u32[]{:S(2)}, u32[]{:S(2)}) collective-permute-start(bf16[256,128]{1,0:T(8,128)(2,1)S(1)} %bitcast.72), channel_id=1, source_target_pairs={{0,508},{4,0},{8,4},{12,8},{16,12},{20,16},{24,20},{28,24},{32,28}... | collective-permute-start | bytes 196616 | tf_op jit(solution)/shard_map/ppermute | solution.py:10
  173.0 8.0 collective-permute-start.10
  176.1 7.4 collective-permute-start.9
Sparse Core Ops, SparseCore 0:
  181.1 1839.3 all-reduce.1
where the time goes:
time: 2030 us
  waiting for transfers between devices  1860 us (92%)
  starting transfers between devices  75.2 us (4%)
  blocking collectives  71.7 us (4%)
    psum x1, waiting for transfers between devices, on_device(): grad_weight = lax.psum(weight_terms, 'rows') * float(node_total) ** (-0.5)  1840 us
    ppermute x16, starting transfers between devices, shifted(): return lax.ppermute(value, axis, pairs)  75.2 us
  transfers between devices with their start and end apart: 17, of which 4 were waited for; matrix products, arithmetic and copies ran while one was open for 0% of the time, Pallas kernels for 0%

commit v1 on v0

--- a/solution.py
+++ b/solution.py
@@ -73,7 +73,9 @@
         agg_full, grad_pre, (((0,), (0,)), ((), ())), preferred_element_type=jnp.float32
     )
     node_total = local_rows * row_count
-    grad_weight = lax.psum(weight_terms, "rows") * float(node_total) ** (-0.5)
+    grad_weight = jnp.sum(lax.all_gather(weight_terms, "rows"), axis=0) * float(node_total) ** (
+        -0.5
+    )
     feat_index = lax.axis_index("feat")
     weight_rows = lax.dynamic_slice_in_dim(weight_full, feat_index * feat_width, feat_width, 0)
     grad_agg = lax.dot_general(

time: 2030 us -> 1130 us (0.56)
  waiting for transfers between devices: 1860 us -> 950 us
    psum x1 -> x0, waiting for transfers between devices: 1840 us -> none  [on_device(): grad_weight = lax.psum(weight_terms, 'rows') * float(node_total) ** (-0.5)]
    all_gather x0 -> x1, waiting for transfers between devices: none -> 942 us  [on_device(): lax.all_gather(weight_terms, 'rows')]
  transfers between devices with their start and end apart: 17 -> 17, of which waited for: 4 -> 6; matrix products, arithmetic and copies ran while one was open for 0% -> 0% of each run, Pallas kernels for 0% -> 0%
where the time goes in v1:
time: 1130 us
  waiting for transfers between devices  950 us (84%)
  starting transfers between devices  72.2 us (6%)
  blocking collectives  72 us (6%)
  other arithmetic  16.5 us (1%)
  between operations  14.4 us (1%)
    all_gather x1, waiting for transfers between devices, on_device(): lax.all_gather(weight_terms, 'rows')  942 us
    ppermute x16, starting transfers between devices, shifted(): return lax.ppermute(value, axis, pairs)  72.2 us
    all_gather x1, blocking collectives, on_device(): panel_full = lax.all_gather(block_values, 'feat', axis=1, tiled=True)  24.6 us
  transfers between devices with their start and end apart: 17, of which 6 were waited for; matrix products, arithmetic and copies ran while one was open for 0% of the time, Pallas kernels for 0%

profile of v1, /device:TPU:0, one launch (start us, length us, event | category | flops | bytes accessed | tf_op | source)
XLA Modules:
  0.0 1129.4 jit_solution(1902118900952483144)
XLA Ops:
  7.2 0.0 copy-start.1
  7.2 0.0 all-gather.3.cloned.1.call-start
  7.2 1.9 collective-permute-start
  9.2 1.9 collective-permute-start.1
  11.1 3.5 collective-permute-start.2
  14.5 2.9 collective-permute-start.3
  17.4 13.8 %collective-permute-start.4 = (bf16[256,128]{1,0:T(8,128)(2,1)}, bf16[256,128]{1,0:T(8,128)(2,1)S(1)}, u32[]{:S(2)}, u32[]{:S(2)}) collective-permute-start(bf16[256,128]{1,0:T(8,128)(2,1)} %param.6), channel_id=1, source_target_pairs={{0,508},{4,0},{8,4},{12,8},{16,12},{20,16},{24,20},{28,24},{32,28}... | collective-permute-start | bytes 196616 | tf_op jit(solution)/shard_map/ppermute | solution.py:10
  31.2 0.7 compare_and_fusion
  32.0 0.1 reshape.107
  32.0 24.6 %all_gather.18 = bf16[2,8,128,128]{3,2,1,0:T(8,128)(2,1)S(1)} all-gather(bf16[2,2,128,128]{3,2,1,0:T(8,128)(2,1)} %param.8), channel_id=1, replica_groups=mesh['rows'=128,'feat'=4] {'feat'}, dimensions={1}, use_global_device_ids=true | all-gather | bytes 655360 | tf_op jit(solution)/shard_map/all_gather | solution.py:61
  56.6 0.7 iota_compare_fusion
  57.4 0.0 collective-permute-done
  57.4 3.6 collective-permute-start.5
  61.0 0.0 collective-permute-done.1
  61.1 2.7 collective-permute-start.6
  63.8 0.0 collective-permute-done.2
  63.8 3.5 collective-permute-start.7
  67.3 0.0 collective-permute-done.3
  67.3 0.0 copy-done.1
  67.3 0.0 collective-permute-done.4
  67.4 0.0 collective-permute-done.5
  67.4 1.2 collective-permute-done.6
  68.7 1.5 collective-permute-done.7
  70.2 0.6 gather_fusion
  70.8 0.0 copy-start
  70.8 0.0 copy-start.2
  70.8 0.4 fusion
  71.2 14.9 %all_gather.19 = bf16[256,512]{1,0:T(8,128)(2,1)S(1)} all-gather(bf16[256,128]{1,0:T(8,128)(2,1)S(1)} %bitcast.80), channel_id=1, replica_groups=mesh['rows'=128,'feat'=4] {'feat'}, dimensions={1}, use_global_device_ids=true | all-gather | bytes 327680 | tf_op jit(solution)/shard_map/all_gather | solution.py:65
  86.1 0.0 copy-done
  86.1 0.0 copy-done.2
  86.1 0.9 fusion.9
  87.0 1.0 fusion.36
  88.0 0.0 all-gather.3.cloned.1.call-update
  88.0 0.1 reshape.102
  88.1 17.1 %all_gather.21 = bf16[512,512]{1,0:T(8,128)(2,1)S(1)} all-gather(bf16[512,128]{1,0:T(8,128)(2,1)S(1)} %copy-done), channel_id=1, replica_groups=mesh['rows'=128,'feat'=4] {'feat'}, dimensions={1}, use_global_device_ids=true | all-gather | bytes 655360 | tf_op jit(solution)/shard_map/all_gather | solution.py:66
  105.2 15.4 %all_gather.20 = bf16[256,512]{1,0:T(8,128)(2,1)S(1)} all-gather(bf16[256,128]{1,0:T(8,128)(2,1)S(1)} %get-tuple-element.13), channel_id=1, replica_groups=mesh['rows'=128,'feat'=4] {'feat'}, dimensions={1}, use_global_device_ids=true | all-gather | bytes 327680 | tf_op jit(solution)/shard_map/all_gather | solution.py:71
  120.6 0.2 convolution_convert_fusion
  120.9 0.4 fusion.3
  121.3 0.1 broadcast_in_dim.43
  121.4 1.6 scatter_fusion
  123.0 0.1 convert.10
  123.2 1.9 collective-permute-start.15
  125.1 7.3 collective-permute-start.14
  132.4 4.1 collective-permute-start.13
  136.6 3.6 collective-permute-start.12
  140.2 14.2 %collective-permute-start.11 = (bf16[256,128]{1,0:T(8,128)(2,1)S(1)}, bf16[256,128]{1,0:T(8,128)(2,1)S(1)}, u32[]{:S(2)}, u32[]{:S(2)}) collective-permute-start(bf16[256,128]{1,0:T(8,128)(2,1)S(1)} %bitcast.75), channel_id=1, source_target_pairs={{0,508},{4,0},{8,4},{12,8},{16,12},{20,16},{24,20},{28,24},{32,28}... | collective-permute-start | bytes 196616 | tf_op jit(solution)/shard_map/ppermute | solution.py:10
  154.4 0.0 collective-permute-done.15
  154.4 3.4 collective-permute-start.10
  157.8 0.0 collective-permute-done.14
  157.8 1.9 collective-permute-start.9
  159.7 0.0 collective-permute-done.13
  159.7 1.9 collective-permute-start.8
  161.7 0.0 collective-permute-done.12
  161.7 0.0 collective-permute-done.11
  161.7 0.6 collective-permute-done.10
  162.3 3.3 collective-permute-done.9
  165.5 1.2 collective-permute-done.8
  166.7 0.7 fusion.24
  167.4 942.4 %all-gather.3.cloned.1.call-done = f32[65536,128]{1,0:T(8,128)} async-done(((f32[512,128]{1,0:T(8,128)}), f32[65536,128]{1,0:T(8,128)}) %all-gather.3.cloned.1.call-update) | async-done | bytes 33554448 | tf_op jit(solution)/shard_map/all_gather | solution.py:76
  1109.8 12.0 %reduce_sum.9 = f32[512,128]{1,0:T(8,128)S(1)} reduce(f32[128,512,128]{2,1,0:T(8,128)} %bitcast.67, f32[]{:T(128)} %constant.84.clone.1), dimensions={0}, to_apply=%region_1.2 | reduce | flops 8323072 | bytes 33816580 | tf_op jit(solution)/shard_map/reduce_sum | solution.py:76
  1121.8 0.7 broadcast_multiply_fusion
  (14 shorter events, 0.2 us)
Async XLA Ops:
  7.2 60.2 %copy-start.1 = (bf16[256,128]{1,0:T(8,128)(2,1)S(1)}, bf16[256,128]{1,0:T(8,128)(2,1)}, u32[]{:S(2)}) copy-start(bf16[256,128]{1,0:T(8,128)(2,1)} %param.6) | copy-start | bytes 196612
  7.2 1102.7 %all-gather.3.cloned.1.call-start = ((), (), s32[]{:S(2)}) async-start(), calls=%async_computation | async-start | bytes 33816576 | tf_op jit(solution)/shard_map/all_gather | solution.py:76
  7.2 50.2 %collective-permute-start = (bf16[256,128]{1,0:T(8,128)(2,1)}, bf16[256,128]{1,0:T(8,128)(2,1)S(1)}, u32[]{:S(2)}, u32[]{:S(2)}) collective-permute-start(bf16[256,128]{1,0:T(8,128)(2,1)} %param.6), channel_id=1, source_target_pairs={{0,16},{4,20},{8,24},{12,28},{16,32},{20,36},{24,40},{28,44},{32,4... | collective-permute-start | bytes 196616 | tf_op jit(solution)/shard_map/ppermute | solution.py:10
  9.2 51.9 %collective-permute-start.1 = (bf16[256,128]{1,0:T(8,128)(2,1)}, bf16[256,128]{1,0:T(8,128)(2,1)S(1)}, u32[]{:S(2)}, u32[]{:S(2)}) collective-permute-start(bf16[256,128]{1,0:T(8,128)(2,1)} %param.6), channel_id=1, source_target_pairs={{0,12},{4,16},{8,20},{12,24},{16,28},{20,32},{24,36},{28,40},{32,4... | collective-permute-start | bytes 196616 | tf_op jit(solution)/shard_map/ppermute | solution.py:10
  11.1 52.7 %collective-permute-start.2 = (bf16[256,128]{1,0:T(8,128)(2,1)}, bf16[256,128]{1,0:T(8,128)(2,1)S(1)}, u32[]{:S(2)}, u32[]{:S(2)}) collective-permute-start(bf16[256,128]{1,0:T(8,128)(2,1)} %param.6), channel_id=1, source_target_pairs={{0,8},{4,12},{8,16},{12,20},{16,24},{20,28},{24,32},{28,36},{32,40... | collective-permute-start | bytes 196616 | tf_op jit(solution)/shard_map/ppermute | solution.py:10
  14.5 52.7 %collective-permute-start.3 = (bf16[256,128]{1,0:T(8,128)(2,1)}, bf16[256,128]{1,0:T(8,128)(2,1)S(1)}, u32[]{:S(2)}, u32[]{:S(2)}) collective-permute-start(bf16[256,128]{1,0:T(8,128)(2,1)} %param.6), channel_id=1, source_target_pairs={{0,4},{4,8},{8,12},{12,16},{16,20},{20,24},{24,28},{28,32},{32,36}... | collective-permute-start | bytes 196616 | tf_op jit(solution)/shard_map/ppermute | solution.py:10
  17.4 49.9 %collective-permute-start.4 = (bf16[256,128]{1,0:T(8,128)(2,1)}, bf16[256,128]{1,0:T(8,128)(2,1)S(1)}, u32[]{:S(2)}, u32[]{:S(2)}) collective-permute-start(bf16[256,128]{1,0:T(8,128)(2,1)} %param.6), channel_id=1, source_target_pairs={{0,508},{4,0},{8,4},{12,8},{16,12},{20,16},{24,20},{28,24},{32,28}... | collective-permute-start | bytes 196616 | tf_op jit(solution)/shard_map/ppermute | solution.py:10
  57.4 10.0 collective-permute-start.5
  61.1 7.6 collective-permute-start.6
  63.8 6.4 collective-permute-start.7
  70.8 15.3 %copy-start = (bf16[512,128]{1,0:T(8,128)(2,1)S(1)}, bf16[512,128]{1,0:T(8,128)(2,1)}, u32[]{:S(2)}) copy-start(bf16[512,128]{1,0:T(8,128)(2,1)} %param.7) | copy-start | bytes 393220
  70.8 15.3 %copy-start.2 = (bf16[256,128]{1,0:T(8,128)(2,1)S(1)}, bf16[256,128]{1,0:T(8,128)(2,1)}, u32[]{:S(2)}) copy-start(bf16[256,128]{1,0:T(8,128)(2,1)} %param.11) | copy-start | bytes 196612
  123.2 31.2 %collective-permute-start.15 = (bf16[256,128]{1,0:T(8,128)(2,1)S(1)}, bf16[256,128]{1,0:T(8,128)(2,1)S(1)}, u32[]{:S(2)}, u32[]{:S(2)}) collective-permute-start(bf16[256,128]{1,0:T(8,128)(2,1)S(1)} %bitcast.79), channel_id=1, source_target_pairs={{0,16},{4,20},{8,24},{12,28},{16,32},{20,36},{24,40},{28,44},{32,4... | collective-permute-start | bytes 196616 | tf_op jit(solution)/shard_map/ppermute | solution.py:10
  125.1 32.7 %collective-permute-start.14 = (bf16[256,128]{1,0:T(8,128)(2,1)S(1)}, bf16[256,128]{1,0:T(8,128)(2,1)S(1)}, u32[]{:S(2)}, u32[]{:S(2)}) collective-permute-start(bf16[256,128]{1,0:T(8,128)(2,1)S(1)} %bitcast.78), channel_id=1, source_target_pairs={{0,12},{4,16},{8,20},{12,24},{16,28},{20,32},{24,36},{28,40},{32,4... | collective-permute-start | bytes 196616 | tf_op jit(solution)/shard_map/ppermute | solution.py:10
  132.4 27.3 %collective-permute-start.13 = (bf16[256,128]{1,0:T(8,128)(2,1)S(1)}, bf16[256,128]{1,0:T(8,128)(2,1)S(1)}, u32[]{:S(2)}, u32[]{:S(2)}) collective-permute-start(bf16[256,128]{1,0:T(8,128)(2,1)S(1)} %bitcast.77), channel_id=1, source_target_pairs={{0,8},{4,12},{8,16},{12,20},{16,24},{20,28},{24,32},{28,36},{32,40... | collective-permute-start | bytes 196616 | tf_op jit(solution)/shard_map/ppermute | solution.py:10
  136.6 25.1 %collective-permute-start.12 = (bf16[256,128]{1,0:T(8,128)(2,1)S(1)}, bf16[256,128]{1,0:T(8,128)(2,1)S(1)}, u32[]{:S(2)}, u32[]{:S(2)}) collective-permute-start(bf16[256,128]{1,0:T(8,128)(2,1)S(1)} %bitcast.76), channel_id=1, source_target_pairs={{0,4},{4,8},{8,12},{12,16},{16,20},{20,24},{24,28},{28,32},{32,36}... | collective-permute-start | bytes 196616 | tf_op jit(solution)/shard_map/ppermute | solution.py:10
  140.2 21.5 %collective-permute-start.11 = (bf16[256,128]{1,0:T(8,128)(2,1)S(1)}, bf16[256,128]{1,0:T(8,128)(2,1)S(1)}, u32[]{:S(2)}, u32[]{:S(2)}) collective-permute-start(bf16[256,128]{1,0:T(8,128)(2,1)S(1)} %bitcast.75), channel_id=1, source_target_pairs={{0,508},{4,0},{8,4},{12,8},{16,12},{20,16},{24,20},{28,24},{32,28}... | collective-permute-start | bytes 196616 | tf_op jit(solution)/shard_map/ppermute | solution.py:10
  154.4 7.9 collective-permute-start.10
  157.8 7.7 collective-permute-start.9
  159.7 7.0 collective-permute-start.8
Sparse Core Ops, SparseCore 0:
  88.1 1021.6 all-gather.2
